TPU v7x, 32 devices: a whole 2x2x4 slice. The times are simulated.
32 devices in a mesh: groups: 2 (over y), patch: 8 (over z, x), head: 2 (over core).
Axes of the slice: x: 2, y: 2, z: 4, core: 2. Of those that a mesh axis runs over, the one named last changes fastest.
Arguments:
- queries: bfloat16 [2, 256, 1536], P(None, ('groups', 'patch'), 'head'), parts along dimension 1, may hold values from -15 to 15
- stale_pairs: bfloat16 [2, 320, 1536], P(None, ('groups', 'patch'), 'head'), parts along dimension 1, may hold values from -6 to 6
- step_pairs: bfloat16 [2, 2, 320, 1536], P(None, None, ('groups', 'patch'), 'head'), parts along dimension 2, may hold values from -6 to 6
- hidden: bfloat16 [256, 3072], P(('groups', 'patch'), 'head'), parts along dimension 0, may hold values from -3 to 3
- out_weight: bfloat16 [1536, 3072], P('head'), may hold values from -0.15625 to 0.15625
- gate_table: bfloat16 [28, 3072], replicated, may hold values from -4 to 4
- t_index: int32 [4], P('groups'), parts along dimension 0, may hold values from 0 to 27
- text_len: int32 [2], P('groups'), parts along dimension 0, may hold values from 1 to 32
Outputs:
- final_latents: bfloat16 [256, 3072], P(('groups', 'patch', 'head')), parts along dimension 0
There are 2 independent parts, one for each index of `groups`. A program takes and returns all parts, laid end to end along the dimension named above; an argument that names none is the same for every part. Nothing has to cross between parts.
All inputs are finite; a program needn't handle non-finite values.
Results may differ from a plain program's by a relative error of at most 0.0065.
Values may be sent and summed in bfloat16 or wider, within the bound.
A program may use at most 128 MiB of HBM per device.

v0:
```python
import jax
import jax.numpy as jnp
from jax import lax
from jax.sharding import PartitionSpec as P

HDIM = 128


def attend(query_rows, key_rows, value_rows, usable):
    count = query_rows.shape[0]
    total = key_rows.shape[0]
    heads_here = query_rows.shape[1] // HDIM
    qs = query_rows.reshape(count, heads_here, HDIM)
    ks = key_rows.reshape(total, heads_here, HDIM)
    vs = value_rows.reshape(total, heads_here, HDIM)
    scores = jnp.einsum("qhd,khd->hqk", qs, ks, preferred_element_type=jnp.float32) * (
        1.0 / HDIM**0.5
    )
    scores = jnp.where(usable[None, None, :], scores, jnp.float32(-1e30))
    top = jnp.max(scores, axis=2, keepdims=True)
    expo = jnp.exp(scores - top)
    weights = (expo / jnp.sum(expo, axis=2, keepdims=True)).astype(jnp.bfloat16)
    mixed = jnp.einsum("hqk,khd->qhd", weights, vs, preferred_element_type=jnp.float32)
    return mixed.reshape(count, heads_here * HDIM).astype(jnp.bfloat16)


def per_device(queries, stale_pairs, step_pairs, hidden, out_weight, gate_table, t_index, text_len):
    strip_rows = stale_pairs.shape[1]
    lat_rows = queries.shape[1]
    text_rows = strip_rows - lat_rows
    strip_count = lax.axis_size("patch")
    strip_index = lax.axis_index("patch")
    head_index = lax.axis_index("head")
    head_count = lax.axis_size("head")
    total = strip_rows * strip_count
    positions = jnp.arange(total, dtype=jnp.int32)
    within = positions % strip_rows
    holder = positions // strip_rows
    usable = (within < lat_rows) | (holder * text_rows + within - lat_rows < text_len[0])
    old_sets = lax.all_gather(stale_pairs, "patch", axis=1, tiled=True)
    first_sets = lax.all_gather(step_pairs[0], "patch", axis=1, tiled=True)
    remote_sets = (old_sets, first_sets)
    model_width = out_weight.shape[1]
    col_width = model_width // head_count

    def project(section):
        pairs = lax.dynamic_update_slice_in_dim(
            remote_sets[section], step_pairs[section], strip_index * strip_rows, axis=1
        )
        attended = attend(queries[section], pairs[0], pairs[1], usable)
        return jnp.dot(attended, out_weight, preferred_element_type=jnp.float32)

    state = hidden.astype(jnp.float32)
    first_proj = lax.psum_scatter(
        project(0).astype(jnp.bfloat16), "head", scatter_dimension=1, tiled=True
    ).astype(jnp.float32)
    gate_row = gate_table[t_index[0]].astype(jnp.float32)
    state = (
        state
        + lax.dynamic_slice_in_dim(gate_row, head_index * col_width, col_width, 0)[None, :]
        * first_proj
    )
    moved = lax.all_to_all(state, "head", split_axis=0, concat_axis=1, tiled=True)
    last_proj = lax.psum_scatter(project(1), "head", scatter_dimension=0, tiled=True)
    gate_full = gate_table[t_index[1]].astype(jnp.float32)
    return (moved + gate_full[None, :] * last_proj).astype(jnp.bfloat16)


def solution(mesh):
    return jax.shard_map(
        per_device,
        mesh=mesh,
        in_specs=(
            P(None, ("groups", "patch"), "head"),
            P(None, ("groups", "patch"), "head"),
            P(None, None, ("groups", "patch"), "head"),
            P(("groups", "patch"), "head"),
            P("head", None),
            P(),
            P("groups"),
            P("groups"),
        ),
        out_specs=P(("groups", "patch", "head"), None),
        check_vma=False,
    )
```

profile of v0, /device:TPU:0, one launch (start us, length us, event | category | flops | bytes accessed | tf_op | source)
XLA Modules:
  0.0 112.2 jit_solution(2523433137556579357)
XLA Ops:
  6.5 0.0 reduce-scatter.3.cloned.1.call-start
  6.5 0.9 slice_bitcast_fusion
  7.4 33.0 %all-gather = bf16[1,2,160,768]{3,1,0,2:T(2,128)(2,1)S(1)} all-gather(bf16[1,2,20,768]{3,1,0,2:T(2,128)(2,1)S(1)} %slice_bitcast_fusion), channel_id=2, replica_groups=mesh['groups'=2,'patch'=8,'head'=2] {'patch'}, dimensions={2}, use_global_device_ids=true | all-gather | bytes 552960 | tf_op jit(solution)/shard_map/all_gather | solution.py:41
  40.4 31.4 %all_gather.6 = bf16[2,160,768]{2,0,1:T(2,128)(2,1)S(1)} all-gather(bf16[2,20,768]{2,0,1:T(2,128)(2,1)} %param.9), channel_id=1, replica_groups=mesh['groups'=2,'patch'=8,'head'=2] {'patch'}, dimensions={1}, use_global_device_ids=true | all-gather | bytes 552960 | tf_op jit(solution)/shard_map/all_gather | solution.py:40
  71.7 0.8 fusion.33
  72.5 0.1 reshape_squeeze.20
  73.2 1.0 bitcast_dynamic-update-slice_fusion
  74.2 5.2 %slice_reduce_fusion.1 = (bf16[160,768]{1,0:T(8,128)(2,1)S(1)}, bf16[160,768]{1,0:T(8,128)(2,1)S(1)}, bf16[160,768]{1,0:T(8,128)(2,1)S(1)}, bf16[160,768]{1,0:T(8,128)(2,1)S(1)}) fusion(bf16[2,160,768]{2,0,1:T(2,128)(2,1)S(1)} %get-tuple-element.9, bf16[2,160,768]{2,0,1:T(2,128)(2,1)S(1)} %get-tuple-element.10), kind=kLoop, calls=%fused_computation.18 | loop fusion | bytes 1966080 | tf_op jit(solution)/shard_map/slice | solution.py:50
  79.3 0.4 fusion.35
  79.8 0.2 fusion.10
  80.0 0.0 copy-start.1
  80.0 0.0 copy-start
  80.0 3.7 %convolution_convert_fusion = bf16[16,3072]{1,0:T(8,128)(2,1)} fusion(bf16[768,3072]{1,0:T(8,128)(2,1)} %param.12, bf16[6,2,8,128]{3,2,1,0:T(8,128)(2,1)S(1)} %fusion.10), kind=kOutput, calls=%fused_computation.2 | convolution fusion | flops 75546624 | bytes 4841472 | tf_op jit(solution)/shard_map/dot_general | solution.py:51
  83.7 0.0 reduce-scatter.3.cloned.1.call-update
  83.8 0.0 reduce-scatter.5.cloned.1.call-start
  83.8 0.1 reshape_squeeze.23
  83.9 0.4 fusion.36
  84.3 0.2 fusion.11
  84.5 3.7 %fusion.22 = f32[16,3072]{1,0:T(8,128)} fusion(bf16[768,3072]{1,0:T(8,128)(2,1)} %param.12, bf16[6,2,8,128]{3,2,1,0:T(8,128)(2,1)S(1)} %fusion.11), kind=kOutput, calls=%fused_computation.38 | convolution fusion | flops 75497472 | bytes 4939776 | tf_op jit(solution)/shard_map/dot_general | solution.py:51
  88.3 0.0 reduce-scatter.5.cloned.1.call-update
  88.3 0.0 copy-done.1
  88.3 0.6 fusion.34
  92.5 0.8 dynamic-slice_convert_fusion
  93.4 0.8 fusion.29
  94.2 0.0 reduce-scatter.3.cloned.1.call-done
  94.2 0.0 copy-done
  94.2 0.8 add_bitcast_fusion
  95.1 3.8 %all_to_all.19 = f32[2,8,1536]{2,1,0:T(8,128)S(1)} all-to-all(f32[2,8,1536]{2,1,0:T(8,128)S(1)} %add_bitcast_fusion), channel_id=1, replica_groups=mesh['groups'=2,'patch'=8,'head'=2] {'head'}, dimensions={0} | all-to-all | bytes 196608 | tf_op jit(solution)/shard_map/all_to_all | solution.py:63
  98.9 5.0 %reduce-scatter.5.cloned.1.call-done = f32[8,3072]{1,0:T(8,128)} async-done(((f32[16,3072]{1,0:T(8,128)}), f32[8,3072]{1,0:T(8,128)}) %reduce-scatter.5.cloned.1.call-update) | async-done | bytes 98320 | tf_op jit(solution)/shard_map/reduce_scatter | solution.py:64
  103.8 1.5 %add_convert_fusion = bf16[8,3072]{1,0:T(8,128)(2,1)} fusion(f32[8,3072]{1,0:T(8,128)S(1)} %bitcast.74, f32[8,3072]{1,0:T(8,128)} %reduce-scatter.5.cloned.1.call-done, f32[3072]{0:T(1024)S(1)} %bitcast.75), kind=kLoop, calls=%fused_computation.29 | loop fusion | flops 73728 | bytes 258048 | tf_op jit(solution)/shard_map/convert_element_type | solution.py:66
  (1 shorter events, 0.0 us)
Async XLA Ops:
  6.5 87.7 %reduce-scatter.3.cloned.1.call-start = ((), (), s32[]{:S(2)}) async-start(), calls=%async_computation.3 | async-start | bytes 147456 | tf_op jit(solution)/shard_map/reduce_scatter | solution.py:54
  80.0 8.3 %copy-start.1 = (s32[2]{0:T(128)S(1)}, s32[2]{0:T(128)}, u32[]{:S(2)}) copy-start(s32[2]{0:T(128)} %param.14) | copy-start | bytes 28
  80.0 14.2 %copy-start = (bf16[16,1536]{1,0:T(8,128)(2,1)S(1)}, bf16[16,1536]{1,0:T(8,128)(2,1)}, u32[]{:S(2)}) copy-start(bf16[16,1536]{1,0:T(8,128)(2,1)} %param.11) | copy-start | bytes 147460
  83.8 20.1 %reduce-scatter.5.cloned.1.call-start = ((), (), s32[]{:S(2)}) async-start(), calls=%async_computation.4 | async-start | bytes 294912 | tf_op jit(solution)/shard_map/reduce_scatter | solution.py:64
Sparse Core Ops, SparseCore 0:
  83.9 8.8 reduce-scatter.2
  95.1 8.7 reduce-scatter.4
where the time goes:
time: 113 us; the launch traced here: 112 us
  blocking collectives  68.1 us (60%)
  between operations  17.8 us (16%)
  matrix products  8.77 us (8%)
  local copies, waits for them, and re-layouts  8.44 us (7%)
  waiting for transfers between devices  5.03 us (4%)
  other arithmetic  4.01 us (4%)
    all_gather x1, blocking collectives, per_device(): first_sets = lax.all_gather(step_pairs[0], 'patch', axis=1, tiled=True)  33 us
    all_gather x1, blocking collectives, per_device(): old_sets = lax.all_gather(stale_pairs, 'patch', axis=1, tiled=True)  31.4 us
    dot_general x2, matrix products, project(): return jnp.dot(attended, out_weight, preferred_element_type=jnp.float32)  7.5 us
    slice x2, local copies, waits for them, and re-layouts, project(): attended = attend(queries[section], pairs[0], pairs[1], usable)  5.91 us
    reduce_scatter x1, waiting for transfers between devices, per_device(): lax.psum_scatter(project(1), 'head', scatter_dimension=0, tiled=True)  4.98 us
    all_to_all x1, blocking collectives, per_device(): lax.all_to_all(state, 'head', split_axis=0, concat_axis=1, tiled=True)  3.79 us
  transfers between devices with their start and end apart: 2, of which 1 were waited for; matrix products, arithmetic and copies ran while one was open for 7% of the time, Pallas kernels for 0%

commit v1 on v0

--- a/solution.py
+++ b/solution.py
@@ -37,7 +37,22 @@
     within = positions % strip_rows
     holder = positions // strip_rows
     usable = (within < lat_rows) | (holder * text_rows + within - lat_rows < text_len[0])
-    old_sets = lax.all_gather(stale_pairs, "patch", axis=1, tiled=True)
+
+    def convert_sheet(mine_x, axis_id):
+        extent = lax.axis_size(axis_id)
+        part_now = mine_x
+        panels = [part_now]
+        work_now = sorted(((q, (q + 1) % extent) for q in range(extent)))
+        for p in range(1, extent):
+            part_now = lax.ppermute(part_now, axis_id, work_now)
+            panels.insert(0, part_now)
+        u1 = jnp.concatenate(panels, axis=1)
+        current_block = lax.axis_index(axis_id)
+        val = current_block + 1
+        f_now = jnp.roll(u1, val * mine_x.shape[1], axis=1)
+        return f_now
+
+    old_sets = convert_sheet(stale_pairs, "patch")
     first_sets = lax.all_gather(step_pairs[0], "patch", axis=1, tiled=True)
     remote_sets = (old_sets, first_sets)
     model_width = out_weight.shape[1]

time: 113 us -> 126 us (1.12)
  waiting for transfers between devices: 5.03 us -> 41.5 us
  blocking collectives: 68.1 us -> 35.4 us
  starting transfers between devices: 0.04 us -> 4.96 us
  local copies, waits for them, and re-layouts: 8.44 us -> 12 us
    ppermute x0 -> x7, waiting for transfers between devices: none -> 32.7 us  [convert_sheet(): part_now = lax.ppermute(part_now, axis_id, work_now)]
    all_gather x1 -> x0, blocking collectives: 31.4 us -> none  [per_device(): old_sets = lax.all_gather(stale_pairs, 'patch', axis=1, tiled=True)]
    ppermute x0 -> x7, starting transfers between devices: none -> 4.92 us  [convert_sheet(): part_now = lax.ppermute(part_now, axis_id, work_now)]
    unnamed x4 -> x18, local copies, waits for them, and re-layouts: 0.01 us -> 2.5 us
    reduce_scatter x1, waiting for transfers between devices: 0.02 us -> 2.3 us  [per_device(): lax.psum_scatter(project(0).astype(jnp.bfloat16), 'head', scatter_dimensi...]
    reduce_scatter x1, waiting for transfers between devices: 4.98 us -> 6.39 us  [per_device(): lax.psum_scatter(project(1), 'head', scatter_dimension=0, tiled=True)]
    all_gather x1, blocking collectives: 33 us -> 31.6 us  [per_device(): first_sets = lax.all_gather(step_pairs[0], 'patch', axis=1, tiled=True)]
  transfers between devices with their start and end apart: 2 -> 9, of which waited for: 1 -> 8; matrix products, arithmetic and copies ran while one was open for 7% -> 8% of each run, Pallas kernels for 0% -> 0%
where the time goes in v1:
time: 126 us; the launch traced here: 125 us
  waiting for transfers between devices  41.5 us (33%)
  blocking collectives  35.4 us (28%)
  between operations  18.2 us (14%)
  local copies, waits for them, and re-layouts  12 us (10%)
  matrix products  8.76 us (7%)
  starting transfers between devices  4.96 us (4%)
  other arithmetic  4.01 us (3%)
    ppermute x7, waiting for transfers between devices, convert_sheet(): part_now = lax.ppermute(part_now, axis_id, work_now)  32.7 us
    all_gather x1, blocking collectives, per_device(): first_sets = lax.all_gather(step_pairs[0], 'patch', axis=1, tiled=True)  31.6 us
    dot_general x2, matrix products, project(): return jnp.dot(attended, out_weight, preferred_element_type=jnp.float32)  7.49 us
    reduce_scatter x1, waiting for transfers between devices, per_device(): lax.psum_scatter(project(1), 'head', scatter_dimension=0, tiled=True)  6.39 us
    slice x2, local copies, waits for them, and re-layouts, project(): attended = attend(queries[section], pairs[0], pairs[1], usable)  5.87 us
    ppermute x7, starting transfers between devices, convert_sheet(): part_now = lax.ppermute(part_now, axis_id, work_now)  4.92 us
    all_to_all x1, blocking collectives, per_device(): lax.all_to_all(state, 'head', split_axis=0, concat_axis=1, tiled=True)  3.79 us
  transfers between devices with their start and end apart: 9, of which 8 were waited for; matrix products, arithmetic and copies ran while one was open for 8% of the time, Pallas kernels for 0%

profile of v1, /device:TPU:0, one launch (start us, length us, event | category | flops | bytes accessed | tf_op | source)
XLA Modules:
  0.0 124.8 jit_solution(5311664434787692759)
XLA Ops:
  6.5 3.0 %collective-permute-start = (bf16[2,20,768]{2,0,1:T(2,128)(2,1)}, bf16[2,20,768]{2,0,1:T(2,128)(2,1)S(1)}, u32[]{:S(2)}, u32[]{:S(2)}) collective-permute-start(bf16[2,20,768]{2,0,1:T(2,128)(2,1)} %param.9), channel_id=1, source_target_pairs={{0,2},{2,4},{4,6},{6,8},{8,10},{10,12},{12,14},{14,0},{1,3},{3,5},... | collective-permute-start | bytes 184328 | tf_op jit(solution)/shard_map/ppermute | solution.py:47
  9.5 5.4 %collective-permute-done = bf16[2,20,768]{2,0,1:T(2,128)(2,1)S(1)} collective-permute-done((bf16[2,20,768]{2,0,1:T(2,128)(2,1)}, bf16[2,20,768]{2,0,1:T(2,128)(2,1)S(1)}, u32[]{:S(2)}, u32[]{:S(2)}) %collective-permute-start) | collective-permute-done | bytes 61472 | tf_op jit(solution)/shard_map/ppermute | solution.py:47
  15.0 1.3 %fusion.34 = (s32[1]{0:T(128)}, s32[1]{0:T(128)}) fusion(s32[2]{0:T(128)} %param.14), kind=kLoop, calls=%fused_computation.75 | loop fusion | bytes 16 | tf_op jit(solution)/shard_map/slice | solution.py:80
  18.2 3.6 %collective-permute-done.1 = bf16[2,20,768]{2,0,1:T(2,128)(2,1)S(1)} collective-permute-done((bf16[2,20,768]{2,0,1:T(2,128)(2,1)S(1)}, bf16[2,20,768]{2,0,1:T(2,128)(2,1)S(1)}, u32[]{:S(2)}, u32[]{:S(2)}) %collective-permute-start.1) | collective-permute-done | bytes 61472 | tf_op jit(solution)/shard_map/ppermute | solution.py:47
  21.9 0.8 dynamic-slice_convert_fusion
  22.7 6.1 %collective-permute-done.2 = bf16[2,20,768]{2,0,1:T(2,128)(2,1)S(1)} collective-permute-done((bf16[2,20,768]{2,0,1:T(2,128)(2,1)S(1)}, bf16[2,20,768]{2,0,1:T(2,128)(2,1)S(1)}, u32[]{:S(2)}, u32[]{:S(2)}) %collective-permute-start.2) | collective-permute-done | bytes 61472 | tf_op jit(solution)/shard_map/ppermute | solution.py:47
  28.8 0.9 slice_bitcast_fusion
  29.7 6.0 %collective-permute-done.3 = bf16[2,20,768]{2,0,1:T(2,128)(2,1)S(1)} collective-permute-done((bf16[2,20,768]{2,0,1:T(2,128)(2,1)S(1)}, bf16[2,20,768]{2,0,1:T(2,128)(2,1)S(1)}, u32[]{:S(2)}, u32[]{:S(2)}) %collective-permute-start.3) | collective-permute-done | bytes 61472 | tf_op jit(solution)/shard_map/ppermute | solution.py:47
  35.7 0.8 fusion.33
  36.5 6.5 %collective-permute-done.4 = bf16[2,20,768]{2,0,1:T(2,128)(2,1)S(1)} collective-permute-done((bf16[2,20,768]{2,0,1:T(2,128)(2,1)S(1)}, bf16[2,20,768]{2,0,1:T(2,128)(2,1)S(1)}, u32[]{:S(2)}, u32[]{:S(2)}) %collective-permute-start.4) | collective-permute-done | bytes 61472 | tf_op jit(solution)/shard_map/ppermute | solution.py:47
  43.0 31.6 %all-gather = bf16[1,2,160,768]{3,1,0,2:T(2,128)(2,1)S(1)} all-gather(bf16[1,2,20,768]{3,1,0,2:T(2,128)(2,1)S(1)} %slice_bitcast_fusion), channel_id=2, replica_groups=mesh['groups'=2,'patch'=8,'head'=2] {'patch'}, dimensions={2}, use_global_device_ids=true | all-gather | bytes 552960 | tf_op jit(solution)/shard_map/all_gather | solution.py:56
  77.4 0.8 fusion.29
  78.3 1.9 %collective-permute-start.6 = (bf16[2,20,768]{2,0,1:T(2,128)(2,1)S(1)}, bf16[2,20,768]{2,0,1:T(2,128)(2,1)S(1)}, u32[]{:S(2)}, u32[]{:S(2)}) collective-permute-start(bf16[2,20,768]{2,0,1:T(2,128)(2,1)S(1)} %collective-permute-done.5), channel_id=1, source_target_pairs={{0,2},{2,4},{4,6},{6,8},{8,10},{10,12},{12,14},{14,0},{1,3},{3,5},... | collective-permute-start | bytes 184328 | tf_op jit(solution)/shard_map/ppermute | solution.py:47
  80.2 5.0 %collective-permute-done.6 = bf16[2,20,768]{2,0,1:T(2,128)(2,1)S(1)} collective-permute-done((bf16[2,20,768]{2,0,1:T(2,128)(2,1)S(1)}, bf16[2,20,768]{2,0,1:T(2,128)(2,1)S(1)}, u32[]{:S(2)}, u32[]{:S(2)}) %collective-permute-start.6) | collective-permute-done | bytes 61472 | tf_op jit(solution)/shard_map/ppermute | solution.py:47
  85.3 0.1 constant_dynamic-update-slice_fusion.14
  85.3 0.1 constant_dynamic-update-slice_fusion.13
  85.6 0.9 constant_dynamic-update-slice_fusion.8
  86.9 0.9 constant_dynamic-update-slice_fusion
  87.8 0.3 constant_dynamic-slice_fusion
  88.2 1.0 bitcast_dynamic-update-slice_fusion.1
  89.2 5.1 %slice_reduce_fusion.1 = (bf16[160,768]{1,0:T(8,128)(2,1)S(1)}, bf16[160,768]{1,0:T(8,128)(2,1)S(1)}, bf16[160,768]{1,0:T(8,128)(2,1)S(1)}, bf16[160,768]{1,0:T(8,128)(2,1)S(1)}) fusion(bf16[2,160,768]{2,0,1:T(2,128)(2,1)S(1)} %get-tuple-element.9, bf16[2,160,768]{2,0,1:T(2,128)(2,1)S(1)} %get-tuple-element.10), kind=kLoop, calls=%fused_computation.18 | loop fusion | bytes 1966080 | tf_op jit(solution)/shard_map/slice | solution.py:65
  94.3 0.4 fusion.35
  94.7 0.2 fusion.10
  94.9 3.7 %convolution_convert_fusion = bf16[16,3072]{1,0:T(8,128)(2,1)} fusion(bf16[768,3072]{1,0:T(8,128)(2,1)} %param.12, bf16[6,2,8,128]{3,2,1,0:T(8,128)(2,1)S(1)} %fusion.10), kind=kOutput, calls=%fused_computation.2 | convolution fusion | flops 75546624 | bytes 4841472 | tf_op jit(solution)/shard_map/dot_general | solution.py:66
  98.7 0.4 fusion.36
  99.1 0.2 fusion.11
  99.4 3.8 %fusion.22 = f32[16,3072]{1,0:T(8,128)} fusion(bf16[768,3072]{1,0:T(8,128)(2,1)} %param.12, bf16[6,2,8,128]{3,2,1,0:T(8,128)(2,1)S(1)} %fusion.11), kind=kOutput, calls=%fused_computation.54 | convolution fusion | flops 75497472 | bytes 4939776 | tf_op jit(solution)/shard_map/dot_general | solution.py:66
  103.1 2.3 %reduce-scatter.3.cloned.1.call-done = bf16[16,1536]{1,0:T(8,128)(2,1)} async-done(((bf16[16,3072]{1,0:T(8,128)(2,1)}), bf16[16,1536]{1,0:T(8,128)(2,1)}) %reduce-scatter.3.cloned.1.call-update) | async-done | bytes 49168 | tf_op jit(solution)/shard_map/reduce_scatter | solution.py:69
  105.4 0.8 add_bitcast_fusion
  106.3 3.8 %all_to_all.19 = f32[2,8,1536]{2,1,0:T(8,128)S(1)} all-to-all(f32[2,8,1536]{2,1,0:T(8,128)S(1)} %add_bitcast_fusion), channel_id=1, replica_groups=mesh['groups'=2,'patch'=8,'head'=2] {'head'}, dimensions={0} | all-to-all | bytes 196608 | tf_op jit(solution)/shard_map/all_to_all | solution.py:78
  110.1 6.4 %reduce-scatter.5.cloned.1.call-done = f32[8,3072]{1,0:T(8,128)} async-done(((f32[16,3072]{1,0:T(8,128)}), f32[8,3072]{1,0:T(8,128)}) %reduce-scatter.5.cloned.1.call-update) | async-done | bytes 98320 | tf_op jit(solution)/shard_map/reduce_scatter | solution.py:79
  116.5 1.5 %add_convert_fusion = bf16[8,3072]{1,0:T(8,128)(2,1)} fusion(f32[8,3072]{1,0:T(8,128)S(1)} %bitcast.75, f32[8,3072]{1,0:T(8,128)} %reduce-scatter.5.cloned.1.call-done, f32[3072]{0:T(1024)S(1)} %bitcast.76), kind=kLoop, calls=%fused_computation.29 | loop fusion | flops 73728 | bytes 258048 | tf_op jit(solution)/shard_map/convert_element_type | solution.py:81
  (27 shorter events, 0.9 us)
Async XLA Ops:
  6.5 98.9 %reduce-scatter.3.cloned.1.call-start = ((), (), s32[]{:S(2)}) async-start(), calls=%async_computation.3 | async-start | bytes 147456 | tf_op jit(solution)/shard_map/reduce_scatter | solution.py:69
  6.5 8.4 %collective-permute-start = (bf16[2,20,768]{2,0,1:T(2,128)(2,1)}, bf16[2,20,768]{2,0,1:T(2,128)(2,1)S(1)}, u32[]{:S(2)}, u32[]{:S(2)}) collective-permute-start(bf16[2,20,768]{2,0,1:T(2,128)(2,1)} %param.9), channel_id=1, source_target_pairs={{0,2},{2,4},{4,6},{6,8},{8,10},{10,12},{12,14},{14,0},{1,3},{3,5},... | collective-permute-start | bytes 184328 | tf_op jit(solution)/shard_map/ppermute | solution.py:47
  15.0 6.9 %collective-permute-start.1 = (bf16[2,20,768]{2,0,1:T(2,128)(2,1)S(1)}, bf16[2,20,768]{2,0,1:T(2,128)(2,1)S(1)}, u32[]{:S(2)}, u32[]{:S(2)}) collective-permute-start(bf16[2,20,768]{2,0,1:T(2,128)(2,1)S(1)} %collective-permute-done), channel_id=1, source_target_pairs={{0,2},{2,4},{4,6},{6,8},{8,10},{10,12},{12,14},{14,0},{1,3},{3,5},... | collective-permute-start | bytes 184328 | tf_op jit(solution)/shard_map/ppermute | solution.py:47
  21.9 6.9 %collective-permute-start.2 = (bf16[2,20,768]{2,0,1:T(2,128)(2,1)S(1)}, bf16[2,20,768]{2,0,1:T(2,128)(2,1)S(1)}, u32[]{:S(2)}, u32[]{:S(2)}) collective-permute-start(bf16[2,20,768]{2,0,1:T(2,128)(2,1)S(1)} %collective-permute-done.1), channel_id=1, source_target_pairs={{0,2},{2,4},{4,6},{6,8},{8,10},{10,12},{12,14},{14,0},{1,3},{3,5},... | collective-permute-start | bytes 184328 | tf_op jit(solution)/shard_map/ppermute | solution.py:47
  28.8 6.9 %collective-permute-start.3 = (bf16[2,20,768]{2,0,1:T(2,128)(2,1)S(1)}, bf16[2,20,768]{2,0,1:T(2,128)(2,1)S(1)}, u32[]{:S(2)}, u32[]{:S(2)}) collective-permute-start(bf16[2,20,768]{2,0,1:T(2,128)(2,1)S(1)} %collective-permute-done.2), channel_id=1, source_target_pairs={{0,2},{2,4},{4,6},{6,8},{8,10},{10,12},{12,14},{14,0},{1,3},{3,5},... | collective-permute-start | bytes 184328 | tf_op jit(solution)/shard_map/ppermute | solution.py:47
  35.7 7.3 %collective-permute-start.4 = (bf16[2,20,768]{2,0,1:T(2,128)(2,1)S(1)}, bf16[2,20,768]{2,0,1:T(2,128)(2,1)S(1)}, u32[]{:S(2)}, u32[]{:S(2)}) collective-permute-start(bf16[2,20,768]{2,0,1:T(2,128)(2,1)S(1)} %collective-permute-done.3), channel_id=1, source_target_pairs={{0,2},{2,4},{4,6},{6,8},{8,10},{10,12},{12,14},{14,0},{1,3},{3,5},... | collective-permute-start | bytes 184328 | tf_op jit(solution)/shard_map/ppermute | solution.py:47
  43.0 35.3 %collective-permute-start.5 = (bf16[2,20,768]{2,0,1:T(2,128)(2,1)S(1)}, bf16[2,20,768]{2,0,1:T(2,128)(2,1)S(1)}, u32[]{:S(2)}, u32[]{:S(2)}) collective-permute-start(bf16[2,20,768]{2,0,1:T(2,128)(2,1)S(1)} %collective-permute-done.4), channel_id=1, source_target_pairs={{0,2},{2,4},{4,6},{6,8},{8,10},{10,12},{12,14},{14,0},{1,3},{3,5},... | collective-permute-start | bytes 184328 | tf_op jit(solution)/shard_map/ppermute | solution.py:47
  78.3 7.0 %collective-permute-start.6 = (bf16[2,20,768]{2,0,1:T(2,128)(2,1)S(1)}, bf16[2,20,768]{2,0,1:T(2,128)(2,1)S(1)}, u32[]{:S(2)}, u32[]{:S(2)}) collective-permute-start(bf16[2,20,768]{2,0,1:T(2,128)(2,1)S(1)} %collective-permute-done.5), channel_id=1, source_target_pairs={{0,2},{2,4},{4,6},{6,8},{8,10},{10,12},{12,14},{14,0},{1,3},{3,5},... | collective-permute-start | bytes 184328 | tf_op jit(solution)/shard_map/ppermute | solution.py:47
  94.9 10.5 %copy-start = (bf16[16,1536]{1,0:T(8,128)(2,1)S(1)}, bf16[16,1536]{1,0:T(8,128)(2,1)}, u32[]{:S(2)}) copy-start(bf16[16,1536]{1,0:T(8,128)(2,1)} %param.11) | copy-start | bytes 147460
  98.7 17.8 %reduce-scatter.5.cloned.1.call-start = ((), (), s32[]{:S(2)}) async-start(), calls=%async_computation.4 | async-start | bytes 294912 | tf_op jit(solution)/shard_map/reduce_scatter | solution.py:79
Sparse Core Ops, SparseCore 0:
  98.8 6.6 reduce-scatter.2
  107.7 8.7 reduce-scatter.4
